TPU v7x, 256 devices: a whole 4x4x8 slice. The times are simulated.
256 devices in a mesh: dp: 128 (over x, y, z), head: 2 (over core).
Axes of the slice: x: 4, y: 4, z: 8, core: 2. Of those that a mesh axis runs over, the one named last changes fastest.
Arguments:
- context: bfloat16 [49152, 2048], P('dp', 'head'), may hold values from -6 to 6
- residual: bfloat16 [49152, 2048], P('dp'), may hold values from -6 to 6
- bias_out: float32 [2048], replicated, may hold values from -3 to 3
- norm_gain: float32 [2048], replicated, may hold values from 0.1 to 1.9
- out_weight: bfloat16 [2048, 2048], P('head', 'dp'), may hold values from -0.125 to 0.125
- cotangent: bfloat16 [49152, 2048], P('dp'), may hold values from -6 to 6
- counts: int32 [128], P('dp'), may hold values from 96 to 384, as said below
- slot_codes: int32 [49152], P('dp'), may hold values from 0 to 383, as said below
Outputs:
- grad_resid: bfloat16 [49152, 2048], P('dp')
- grad_ctx: bfloat16 [49152, 2048], P('dp', 'head')
- grad_wout: float32 [2048, 2048], P('head', 'dp')
Inputs may be any that keep to these rules, and one draw needn't show every extreme that they name: `counts`: one dp index has 384 live rows, every other between 96 and 192. `slot_codes`: the codes of one device are distinct; code c names decoder owner c // 3 and slot c % 3; on every device the first 3 rows go to one owner.
All inputs are finite; a program needn't handle non-finite values.
Results may differ from a plain program's by a relative error of at most 0.0049.
Values may be sent and summed in bfloat16 or wider, within the bound.
No kernel may reach another device: no remote copies, remote signals or barrier semaphores. Data moves between devices by JAX's collectives and lax.ppermute only.
A program may use at most 64 MiB of HBM per device.

v0:
```python
import jax
import jax.numpy as jnp
from jax import lax
from jax.sharding import Mesh, PartitionSpec as P

F32 = jnp.float32
BF16 = jnp.bfloat16


def norm_back(projected, residual, bias_out, norm_gain, grad_out):
    summed_in = residual.astype(F32) + projected + bias_out
    mean_in = jnp.mean(summed_in, axis=-1, keepdims=True)
    centred = summed_in - mean_in
    variance = jnp.mean(centred * centred, axis=-1, keepdims=True)
    inv_std = lax.rsqrt(variance + 1e-05)
    normed = centred * inv_std
    grad_norm = grad_out.astype(F32) * norm_gain
    first_mean = jnp.mean(grad_norm, axis=-1, keepdims=True)
    second_mean = jnp.mean(grad_norm * normed, axis=-1, keepdims=True)
    return (inv_std * (grad_norm - first_mean - normed * second_mean)).astype(BF16)


def shards(context, residual, bias_out, norm_gain, out_weight, cotangent, counts, slot_codes):
    capacity = slot_codes.shape[0]
    features = residual.shape[1]
    half = features // 2
    core = lax.axis_index("core")
    live_mask = jnp.arange(capacity) < counts[0]
    swap = [(0, 1), (1, 0)]
    mine = lax.dynamic_slice_in_dim(cotangent, core * half, half, axis=1)
    returned = lax.all_to_all(mine, ("x", "y", "z"), split_axis=0, concat_axis=0, tiled=True)
    picked = jnp.take(returned, slot_codes, axis=0)
    picked = jnp.where(live_mask[:, None], picked, jnp.zeros((), picked.dtype))
    other = lax.ppermute(picked, "core", swap)
    grad_out = jnp.where(
        core == 0,
        jnp.concatenate([picked, other], axis=1),
        jnp.concatenate([other, picked], axis=1),
    )
    weight_t = lax.all_gather(out_weight.T, "z", axis=0, tiled=True)
    weight_t = lax.all_gather(weight_t, ("x", "y"), axis=0, tiled=True)
    partial_proj = lax.dot_general(
        context, weight_t, (((1,), (1,)), ((), ())), preferred_element_type=F32
    )
    projected = partial_proj + lax.ppermute(partial_proj, "core", swap)
    grad_resid = norm_back(projected, residual, bias_out, norm_gain, grad_out)
    share = lax.dot_general(
        grad_resid, context, (((0,), (0,)), ((), ())), preferred_element_type=F32
    ).astype(BF16)
    grad_ctx = jnp.dot(grad_resid, weight_t, preferred_element_type=F32).astype(BF16)
    total = None
    for axis in ("x", "y", "z"):
        ways = lax.axis_size(axis)
        share = share.reshape(ways, -1, share.shape[-1])
        got = lax.all_to_all(share, axis, split_axis=0, concat_axis=0)
        total = jnp.sum(got.astype(F32), axis=0)
        share = total.astype(BF16)
    replicas = lax.axis_size("x") * lax.axis_size("y") * lax.axis_size("z")
    grad_wout = (total / replicas).T
    return (grad_resid, grad_ctx, grad_wout)


def solution(mesh):
    torus = Mesh(mesh.devices.reshape(4, 4, 8, 2), ("x", "y", "z", "core"))
    dp = ("x", "y", "z")
    return jax.shard_map(
        shards,
        mesh=torus,
        in_specs=(P(dp, "core"), P(dp, None), P(), P(), P("core", dp), P(dp, None), P(dp), P(dp)),
        out_specs=(P(dp, None), P(dp, "core"), P("core", dp)),
        check_vma=False,
    )
```

profile of v0, /device:TPU:2, one launch (start us, length us, event | category | flops | bytes accessed | tf_op | source)
XLA Modules:
  0.0 257.1 jit_solution(9456713248749015484)
XLA Ops:
  7.2 30.8 %all_gather.6 = bf16[128,1024]{1,0:T(8,128)(2,1)} all-gather(bf16[16,1024]{1,0:T(8,128)(2,1)} %bitcast.16), channel_id=1, replica_groups=mesh['x'=4,'y'=4,'z'=8,'core'=2] {'z'}, dimensions={0}, use_global_device_ids=true | all-gather | bytes 294912 | tf_op jit(solution)/shard_map/all_gather | solution.py:40
  38.0 56.2 %all-gather.2.cloned.1.call-done = bf16[2048,1024]{1,0:T(8,128)(2,1)} async-done(((bf16[128,1024]{1,0:T(8,128)(2,1)}), bf16[2048,1024]{1,0:T(8,128)(2,1)}) %all-gather.2.cloned.1.call-update) | async-done | bytes 4194320 | tf_op jit(solution)/shard_map/all_gather | solution.py:41
  94.2 5.9 %fusion.2 = f32[384,2048]{1,0:T(8,128)} fusion(bf16[384,1024]{1,0:T(8,128)(2,1)} %param.8, bf16[2048,1024]{1,0:T(8,128)(2,1)} %all-gather.2.cloned.1.call-done), kind=kOutput, calls=%fused_computation.23 | convolution fusion | flops 1610612736 | bytes 8126464 | tf_op jit(solution)/shard_map/dot_general | solution.py:42
  100.2 1.3 all_to_all.17
  101.5 12.3 %all-to-all-start = ((bf16[128,3,1024]{2,1,0:T(4,128)(2,1)}), bf16[128,3,1024]{2,1,0:T(4,128)(2,1)S(1)}, u32[]{:S(2)}, u32[]{:S(2)}) async-start(bf16[128,3,1024]{2,1,0:T(4,128)(2,1)} %all_to_all.17), calls=%async_computation | async-start | bytes 2097152 | tf_op jit(solution)/shard_map/all_to_all | solution.py:31
  114.5 29.3 %all-to-all-done = bf16[128,3,1024]{2,1,0:T(4,128)(2,1)S(1)} async-done(((bf16[128,3,1024]{2,1,0:T(4,128)(2,1)}), bf16[128,3,1024]{2,1,0:T(4,128)(2,1)S(1)}, u32[]{:S(2)}, u32[]{:S(2)}) %all-to-all-start) | async-done | bytes 786464 | tf_op jit(solution)/shard_map/all_to_all | solution.py:31
  143.9 0.7 all_to_all.19
  144.6 2.1 gather_fusion
  146.6 0.2 select_select_fusion
  146.8 0.1 collective-permute-start.1
  146.9 3.9 %fusion.1 = (f32[384]{0:T(512)S(1)}, f32[384,2048]{1,0:T(8,128)S(1)}) fusion(f32[2048]{0:T(1024)S(1)} %copy-done.4, f32[384,2048]{1,0:T(8,128)} %fusion.2, f32[384,2048]{1,0:T(8,128)} %collective-permute-done, bf16[384,2048]{1,0:T(8,128)(2,1)} %param.9), kind=kLoop, calls=%fused_computation.22 | loop fusion | flops 3931776 | bytes 11019776 | tf_op jit(solution)/shard_map/reduce_sum | solution.py:12
  150.8 0.5 multiply_reduce_fusion.1
  151.3 0.2 copy-done.2
  151.5 1.0 fusion
  152.6 1.6 multiply_convert_fusion
  154.2 2.4 convolution_convert_fusion
  156.6 55.0 %all_to_all.27 = bf16[4,512,1024]{2,1,0:T(8,128)(2,1)} all-to-all(bf16[4,512,1024]{2,1,0:T(8,128)(2,1)S(1)} %bitcast.14), channel_id=1, replica_groups=mesh['x'=4,'y'=4,'z'=8,'core'=2] {'x'}, dimensions={0} | all-to-all | bytes 8388608 | tf_op jit(solution)/shard_map/all_to_all | solution.py:55
  211.6 4.5 %reduce_sum.73 = bf16[512,1024]{1,0:T(8,128)(2,1)} reduce(bf16[4,512,1024]{2,1,0:T(8,128)(2,1)} %all_to_all.27, bf16[]{:T(256)} %constant.40.clone.1), dimensions={0}, to_apply=%region_4.5 | reduce | flops 1572864 | bytes 5242882 | tf_op jit(solution)/shard_map/reduce_sum | solution.py:56
  216.1 18.4 %all_to_all.28 = bf16[4,128,1024]{2,1,0:T(8,128)(2,1)S(1)} all-to-all(bf16[4,128,1024]{2,1,0:T(8,128)(2,1)} %bitcast.15), channel_id=1, replica_groups=mesh['x'=4,'y'=4,'z'=8,'core'=2] {'y'}, dimensions={0} | all-to-all | bytes 2097152 | tf_op jit(solution)/shard_map/all_to_all | solution.py:55
  234.5 0.9 reduce_sum.74
  235.4 3.4 %all-to-all-start.3 = ((bf16[8,16,1024]{2,1,0:T(8,128)(2,1)}), bf16[8,16,1024]{2,1,0:T(8,128)(2,1)S(1)}, u32[]{:S(2)}, u32[]{:S(2)}) async-start(bf16[8,16,1024]{2,1,0:T(8,128)(2,1)} %bitcast.4), calls=%async_computation.3 | async-start | bytes 524288 | tf_op jit(solution)/shard_map/all_to_all | solution.py:55
  238.9 5.3 %convolution_convert_fusion.1 = bf16[384,1024]{1,0:T(8,128)(2,1)} fusion(bf16[384,2048]{1,0:T(8,128)(2,1)} %copy-done.1, bf16[2048,1024]{1,0:T(8,128)(2,1)} %all-gather.2.cloned.1.call-done), kind=kOutput, calls=%fused_computation.9 | convolution fusion | flops 1611005952 | bytes 6553600 | tf_op jit(solution)/shard_map/dot_general | solution.py:50
  244.2 5.4 %all-to-all-done.3 = bf16[8,16,1024]{2,1,0:T(8,128)(2,1)S(1)} async-done(((bf16[8,16,1024]{2,1,0:T(8,128)(2,1)}), bf16[8,16,1024]{2,1,0:T(8,128)(2,1)S(1)}, u32[]{:S(2)}, u32[]{:S(2)}) %all-to-all-start.3) | async-done | bytes 262176 | tf_op jit(solution)/shard_map/all_to_all | solution.py:55
  249.6 0.6 multiply_bitcast_fusion
  (25 shorter events, 0.2 us)
Async XLA Ops:
  7.2 93.0 %copy-start = (bf16[384,2048]{1,0:T(8,128)(2,1)S(1)}, bf16[384,2048]{1,0:T(8,128)(2,1)}, u32[]{:S(2)}) copy-start(bf16[384,2048]{1,0:T(8,128)(2,1)} %param.13) | copy-start | bytes 4718596
  7.2 87.0 %all-gather.2.cloned.1.call-start = ((), (), s32[]{:S(2)}) async-start(), calls=%async_computation.4 | async-start | bytes 4456448 | tf_op jit(solution)/shard_map/all_gather | solution.py:41
  100.1 14.4 %copy-start.3 = (s32[384]{0:T(512)S(1)}, s32[384]{0:T(512)}, u32[]{:S(2)}) copy-start(s32[384]{0:T(512)} %param.15) | copy-start | bytes 4612
  100.1 46.8 %collective-permute-start = (f32[384,2048]{1,0:T(8,128)}, f32[384,2048]{1,0:T(8,128)}, u32[]{:S(2)}, u32[]{:S(2)}) collective-permute-start(f32[384,2048]{1,0:T(8,128)} %fusion.2), channel_id=1, source_target_pairs={{0,1},{1,0},{2,3},{3,2},{4,5},{5,4},{6,7},{7,6},{8,9},{9,8},{10,11... | collective-permute-start | bytes 9437192 | tf_op jit(solution)/shard_map/ppermute | solution.py:45
  101.5 42.4 %all-to-all-start = ((bf16[128,3,1024]{2,1,0:T(4,128)(2,1)}), bf16[128,3,1024]{2,1,0:T(4,128)(2,1)S(1)}, u32[]{:S(2)}, u32[]{:S(2)}) async-start(bf16[128,3,1024]{2,1,0:T(4,128)(2,1)} %all_to_all.17), calls=%async_computation | async-start | bytes 2097152 | tf_op jit(solution)/shard_map/all_to_all | solution.py:31
  144.5 2.4 copy-start.4
  146.8 4.5 %collective-permute-start.1 = (bf16[384,1024]{1,0:T(8,128)(2,1)S(1)}, bf16[384,1024]{1,0:T(8,128)(2,1)S(1)}, u32[]{:S(2)}, u32[]{:S(2)}) collective-permute-start(bf16[384,1024]{1,0:T(8,128)(2,1)S(1)} %select_select_fusion), channel_id=1, source_target_pairs={{0,1},{1,0},{2,3},{3,2},{4,5},{5,4},{6,7},{7,6},{8,9},{9,8},{10,11... | collective-permute-start | bytes 2359304 | tf_op jit(solution)/shard_map/ppermute | solution.py:34
  150.8 0.7 copy-start.2
  152.5 1.6 copy-start.5
  154.2 2.4 copy-start.1
  235.4 14.1 %all-to-all-start.3 = ((bf16[8,16,1024]{2,1,0:T(8,128)(2,1)}), bf16[8,16,1024]{2,1,0:T(8,128)(2,1)S(1)}, u32[]{:S(2)}, u32[]{:S(2)}) async-start(bf16[8,16,1024]{2,1,0:T(8,128)(2,1)} %bitcast.4), calls=%async_computation.3 | async-start | bytes 524288 | tf_op jit(solution)/shard_map/all_to_all | solution.py:55
Sparse Core Ops, SparseCore 0:
  38.1 55.9 all-gather.1
where the time goes:
time: 258 us; the launch traced here: 257 us
  blocking collectives  104 us (40%)
  waiting for transfers between devices  90.9 us (35%)
  starting transfers between devices  15.9 us (6%)
  between operations  14.9 us (6%)
  matrix products  13.7 us (5%)
  other arithmetic  13.2 us (5%)
  local copies, waits for them, and re-layouts  4.35 us (2%)
    all_to_all x2, blocking collectives, shards(): got = lax.all_to_all(share, axis, split_axis=0, concat_axis=0)  73.4 us
    all_gather x1, waiting for transfers between devices, shards(): weight_t = lax.all_gather(weight_t, ('x', 'y'), axis=0, tiled=True)  56.2 us
    all_gather x1, blocking collectives, shards(): weight_t = lax.all_gather(out_weight.T, 'z', axis=0, tiled=True)  30.8 us
    all_to_all x1, waiting for transfers between devices, shards(): lax.all_to_all(mine, ('x', 'y', 'z'), split_axis=0, concat_axis=0, tiled=...  29.3 us
    all_to_all x1, starting transfers between devices, shards(): lax.all_to_all(mine, ('x', 'y', 'z'), split_axis=0, concat_axis=0, tiled=...  12.3 us
    dot_general x1, matrix products, shards(): lax.dot_general(context, weight_t, (((1,), (1,)), ((), ())), preferred_el...  5.94 us
    reduce_sum x3, other arithmetic, shards(): total = jnp.sum(got.astype(F32), axis=0)  5.44 us
    all_to_all x1, waiting for transfers between devices, shards(): got = lax.all_to_all(share, axis, split_axis=0, concat_axis=0)  5.39 us
  transfers between devices with their start and end apart: 5, of which 3 were waited for; matrix products, arithmetic and copies ran while one was open for 5% of the time, Pallas kernels for 0%

commit v1 on v0

--- a/solution.py
+++ b/solution.py
@@ -5,6 +5,18 @@
 
 F32 = jnp.float32
 BF16 = jnp.bfloat16
+
+
+def return_all_flows(mine_x, lane_axis):
+    return jnp.concatenate(
+        lax.all_to_all(
+            jnp.stack([mine_x] * lax.axis_size(lane_axis), axis=0),
+            axis_name=lane_axis,
+            split_axis=0,
+            concat_axis=0,
+        ),
+        0,
+    )
 
 
 def norm_back(projected, residual, bias_out, norm_gain, grad_out):
@@ -37,7 +49,7 @@
         jnp.concatenate([picked, other], axis=1),
         jnp.concatenate([other, picked], axis=1),
     )
-    weight_t = lax.all_gather(out_weight.T, "z", axis=0, tiled=True)
+    weight_t = return_all_flows(out_weight.T, "z")
     weight_t = lax.all_gather(weight_t, ("x", "y"), axis=0, tiled=True)
     partial_proj = lax.dot_general(
         context, weight_t, (((1,), (1,)), ((), ())), preferred_element_type=F32

time: 258 us -> 245 us (0.950)
  blocking collectives: 104 us -> 93.7 us
  waiting for transfers between devices: 90.9 us -> 87.8 us
    all_gather x1 -> x0, blocking collectives: 30.8 us -> none  [shards(): weight_t = lax.all_gather(out_weight.T, 'z', axis=0, tiled=True)]
    all_to_all x0 -> x1, blocking collectives: none -> 20.2 us  [return_all_flows(): lax.all_to_all(jnp.stack([mine_x] * lax.axis_size(lane_axis), axis=0), ax...]
    all_gather x1, waiting for transfers between devices: 56.2 us -> 53 us  [shards(): weight_t = lax.all_gather(weight_t, ('x', 'y'), axis=0, tiled=True)]
where the time goes in v1:
time: 245 us; the launch traced here: 244 us
  blocking collectives  93.7 us (38%)
  waiting for transfers between devices  87.8 us (36%)
  starting transfers between devices  15.9 us (6%)
  between operations  14.9 us (6%)
  matrix products  13.7 us (6%)
  other arithmetic  13.2 us (5%)
  local copies, waits for them, and re-layouts  5.24 us (2%)
    all_to_all x2, blocking collectives, shards(): got = lax.all_to_all(share, axis, split_axis=0, concat_axis=0)  73.4 us
    all_gather x1, waiting for transfers between devices, shards(): weight_t = lax.all_gather(weight_t, ('x', 'y'), axis=0, tiled=True)  53 us
    all_to_all x1, waiting for transfers between devices, shards(): lax.all_to_all(mine, ('x', 'y', 'z'), split_axis=0, concat_axis=0, tiled=...  29.3 us
    all_to_all x1, blocking collectives, return_all_flows(): lax.all_to_all(jnp.stack([mine_x] * lax.axis_size(lane_axis), axis=0), ax...  20.2 us
    all_to_all x1, starting transfers between devices, shards(): lax.all_to_all(mine, ('x', 'y', 'z'), split_axis=0, concat_axis=0, tiled=...  12.3 us
    dot_general x1, matrix products, shards(): lax.dot_general(context, weight_t, (((1,), (1,)), ((), ())), preferred_el...  5.94 us
    reduce_sum x3, other arithmetic, shards(): total = jnp.sum(got.astype(F32), axis=0)  5.44 us
    all_to_all x1, waiting for transfers between devices, shards(): got = lax.all_to_all(share, axis, split_axis=0, concat_axis=0)  5.39 us
  transfers between devices with their start and end apart: 5, of which 3 were waited for; matrix products, arithmetic and copies ran while one was open for 5% of the time, Pallas kernels for 0%

profile of v1, /device:TPU:2, one launch (start us, length us, event | category | flops | bytes accessed | tf_op | source)
XLA Modules:
  0.0 244.4 jit_solution(16088305914626195969)
XLA Ops:
  7.2 0.9 stack.2
  8.1 20.2 %all_to_all.32 = bf16[8,16,1024]{2,1,0:T(8,128)(2,1)} all-to-all(bf16[8,16,1024]{2,1,0:T(8,128)(2,1)S(1)} %stack.2), channel_id=1, replica_groups=mesh['x'=4,'y'=4,'z'=8,'core'=2] {'z'}, dimensions={0} | all-to-all | bytes 524288 | tf_op jit(solution)/shard_map/all_to_all | solution.py:12
  28.4 53.0 %all-gather.2.cloned.1.call-done = bf16[2048,1024]{1,0:T(8,128)(2,1)} async-done(((bf16[128,1024]{1,0:T(8,128)(2,1)}), bf16[2048,1024]{1,0:T(8,128)(2,1)}) %all-gather.2.cloned.1.call-update) | async-done | bytes 4194320 | tf_op jit(solution)/shard_map/all_gather | solution.py:53
  81.4 5.9 %fusion.2 = f32[384,2048]{1,0:T(8,128)} fusion(bf16[384,1024]{1,0:T(8,128)(2,1)} %param.8, bf16[2048,1024]{1,0:T(8,128)(2,1)} %all-gather.2.cloned.1.call-done), kind=kOutput, calls=%fused_computation.23 | convolution fusion | flops 1610612736 | bytes 8126464 | tf_op jit(solution)/shard_map/dot_general | solution.py:54
  87.4 1.3 all_to_all.21
  88.7 12.3 %all-to-all-start.1 = ((bf16[128,3,1024]{2,1,0:T(4,128)(2,1)}), bf16[128,3,1024]{2,1,0:T(4,128)(2,1)S(1)}, u32[]{:S(2)}, u32[]{:S(2)}) async-start(bf16[128,3,1024]{2,1,0:T(4,128)(2,1)} %all_to_all.21), calls=%async_computation.1 | async-start | bytes 2097152 | tf_op jit(solution)/shard_map/all_to_all | solution.py:43
  101.8 29.3 %all-to-all-done.1 = bf16[128,3,1024]{2,1,0:T(4,128)(2,1)S(1)} async-done(((bf16[128,3,1024]{2,1,0:T(4,128)(2,1)}), bf16[128,3,1024]{2,1,0:T(4,128)(2,1)S(1)}, u32[]{:S(2)}, u32[]{:S(2)}) %all-to-all-start.1) | async-done | bytes 786464 | tf_op jit(solution)/shard_map/all_to_all | solution.py:43
  131.1 0.7 all_to_all.23
  131.8 2.1 gather_fusion
  133.9 0.2 select_select_fusion
  134.2 3.9 %fusion.1 = (f32[384]{0:T(512)S(1)}, f32[384,2048]{1,0:T(8,128)S(1)}) fusion(f32[2048]{0:T(1024)S(1)} %copy-done.4, f32[384,2048]{1,0:T(8,128)} %fusion.2, f32[384,2048]{1,0:T(8,128)} %collective-permute-done, bf16[384,2048]{1,0:T(8,128)(2,1)} %param.9), kind=kLoop, calls=%fused_computation.22 | loop fusion | flops 3931776 | bytes 11019776 | tf_op jit(solution)/shard_map/reduce_sum | solution.py:24
  138.1 0.5 multiply_reduce_fusion.1
  138.5 0.2 copy-done.2
  138.7 1.0 fusion
  139.8 1.6 multiply_convert_fusion
  141.4 2.4 convolution_convert_fusion
  143.8 55.0 %all_to_all.33 = bf16[4,512,1024]{2,1,0:T(8,128)(2,1)} all-to-all(bf16[4,512,1024]{2,1,0:T(8,128)(2,1)S(1)} %bitcast.15), channel_id=1, replica_groups=mesh['x'=4,'y'=4,'z'=8,'core'=2] {'x'}, dimensions={0} | all-to-all | bytes 8388608 | tf_op jit(solution)/shard_map/all_to_all | solution.py:67
  198.9 4.5 %reduce_sum.73 = bf16[512,1024]{1,0:T(8,128)(2,1)} reduce(bf16[4,512,1024]{2,1,0:T(8,128)(2,1)} %all_to_all.33, bf16[]{:T(256)} %constant.40.clone.1), dimensions={0}, to_apply=%region_4.5 | reduce | flops 1572864 | bytes 5242882 | tf_op jit(solution)/shard_map/reduce_sum | solution.py:68
  203.3 18.4 %all_to_all.34 = bf16[4,128,1024]{2,1,0:T(8,128)(2,1)S(1)} all-to-all(bf16[4,128,1024]{2,1,0:T(8,128)(2,1)} %bitcast.16), channel_id=1, replica_groups=mesh['x'=4,'y'=4,'z'=8,'core'=2] {'y'}, dimensions={0} | all-to-all | bytes 2097152 | tf_op jit(solution)/shard_map/all_to_all | solution.py:67
  221.8 0.9 reduce_sum.74
  222.7 3.4 %all-to-all-start.4 = ((bf16[8,16,1024]{2,1,0:T(8,128)(2,1)}), bf16[8,16,1024]{2,1,0:T(8,128)(2,1)S(1)}, u32[]{:S(2)}, u32[]{:S(2)}) async-start(bf16[8,16,1024]{2,1,0:T(8,128)(2,1)} %bitcast.5), calls=%async_computation.4 | async-start | bytes 524288 | tf_op jit(solution)/shard_map/all_to_all | solution.py:67
  226.1 5.3 %convolution_convert_fusion.1 = bf16[384,1024]{1,0:T(8,128)(2,1)} fusion(bf16[384,2048]{1,0:T(8,128)(2,1)} %copy-done.1, bf16[2048,1024]{1,0:T(8,128)(2,1)} %all-gather.2.cloned.1.call-done), kind=kOutput, calls=%fused_computation.9 | convolution fusion | flops 1611005952 | bytes 6553600 | tf_op jit(solution)/shard_map/dot_general | solution.py:62
  231.4 5.4 %all-to-all-done.4 = bf16[8,16,1024]{2,1,0:T(8,128)(2,1)S(1)} async-done(((bf16[8,16,1024]{2,1,0:T(8,128)(2,1)}), bf16[8,16,1024]{2,1,0:T(8,128)(2,1)S(1)}, u32[]{:S(2)}, u32[]{:S(2)}) %all-to-all-start.4) | async-done | bytes 262176 | tf_op jit(solution)/shard_map/all_to_all | solution.py:67
  236.9 0.6 multiply_bitcast_fusion
  (26 shorter events, 0.3 us)
Async XLA Ops:
  7.2 80.2 %copy-start = (bf16[384,2048]{1,0:T(8,128)(2,1)S(1)}, bf16[384,2048]{1,0:T(8,128)(2,1)}, u32[]{:S(2)}) copy-start(bf16[384,2048]{1,0:T(8,128)(2,1)} %param.13) | copy-start | bytes 4718596
  7.2 74.2 %all-gather.2.cloned.1.call-start = ((), (), s32[]{:S(2)}) async-start(), calls=%async_computation.5 | async-start | bytes 4456448 | tf_op jit(solution)/shard_map/all_gather | solution.py:53
  87.3 14.4 %copy-start.3 = (s32[384]{0:T(512)S(1)}, s32[384]{0:T(512)}, u32[]{:S(2)}) copy-start(s32[384]{0:T(512)} %param.15) | copy-start | bytes 4612
  87.4 46.8 %collective-permute-start = (f32[384,2048]{1,0:T(8,128)}, f32[384,2048]{1,0:T(8,128)}, u32[]{:S(2)}, u32[]{:S(2)}) collective-permute-start(f32[384,2048]{1,0:T(8,128)} %fusion.2), channel_id=1, source_target_pairs={{0,1},{1,0},{2,3},{3,2},{4,5},{5,4},{6,7},{7,6},{8,9},{9,8},{10,11... | collective-permute-start | bytes 9437192 | tf_op jit(solution)/shard_map/ppermute | solution.py:57
  88.7 42.4 %all-to-all-start.1 = ((bf16[128,3,1024]{2,1,0:T(4,128)(2,1)}), bf16[128,3,1024]{2,1,0:T(4,128)(2,1)S(1)}, u32[]{:S(2)}, u32[]{:S(2)}) async-start(bf16[128,3,1024]{2,1,0:T(4,128)(2,1)} %all_to_all.21), calls=%async_computation.1 | async-start | bytes 2097152 | tf_op jit(solution)/shard_map/all_to_all | solution.py:43
  131.8 2.4 copy-start.4
  134.1 4.5 %collective-permute-start.1 = (bf16[384,1024]{1,0:T(8,128)(2,1)S(1)}, bf16[384,1024]{1,0:T(8,128)(2,1)S(1)}, u32[]{:S(2)}, u32[]{:S(2)}) collective-permute-start(bf16[384,1024]{1,0:T(8,128)(2,1)S(1)} %select_select_fusion), channel_id=1, source_target_pairs={{0,1},{1,0},{2,3},{3,2},{4,5},{5,4},{6,7},{7,6},{8,9},{9,8},{10,11... | collective-permute-start | bytes 2359304 | tf_op jit(solution)/shard_map/ppermute | solution.py:46
  138.0 0.7 copy-start.2
  139.8 1.6 copy-start.5
  141.4 2.4 copy-start.1
  222.7 14.1 %all-to-all-start.4 = ((bf16[8,16,1024]{2,1,0:T(8,128)(2,1)}), bf16[8,16,1024]{2,1,0:T(8,128)(2,1)S(1)}, u32[]{:S(2)}, u32[]{:S(2)}) async-start(bf16[8,16,1024]{2,1,0:T(8,128)(2,1)} %bitcast.5), calls=%async_computation.4 | async-start | bytes 524288 | tf_op jit(solution)/shard_map/all_to_all | solution.py:67
Sparse Core Ops, SparseCore 0:
  28.5 52.8 all-gather.1
